TPU v7x, 512 devices: a whole 4x8x8 slice. The times are simulated.
512 devices in a mesh: vox: 32 (over z_lo, y), opt: 16 (over z_hi, x, core).
Axes of the slice: x: 4, y: 8, z: 8 (z_hi: 2, z_lo: 4; z = z_hi * 4 + z_lo), core: 2. Of those that a mesh axis runs over, the one named last changes fastest.
Arguments:
- source_fields: bfloat16 [1024, 24576], P('opt', 'vox'), may hold values from -6 to 6
- detector_fields: bfloat16 [4096, 24576], P('opt', 'vox'), may hold values from -6 to 6
- measured: float32 [1024, 4096], P('vox', 'opt'), may hold values from -6 to 6
- valid_pair: int32 [1024, 4096], P('vox', 'opt'), may hold values 0 or 1
- weight_class: int32 [1024, 4096], P('vox', 'opt'), may hold values from 0 to 3
- absorption: float32 [24576], P('vox'), may hold values from 0 to 1
Outputs:
- absorption_out: float32 [24576], P('vox')
- residual_out: float32 [1024, 4096], P('vox', 'opt')
All inputs are finite; a program needn't handle non-finite values. No bound on the sum of `valid_pair` on one device may be relied on, other than what follows from the above.
Results may differ from a plain program's by a relative error of at most 0.0026.
Values may be sent and summed in bfloat16 or wider, within the bound.
No kernel may reach another device: no remote copies, remote signals or barrier semaphores. Data moves between devices by JAX's collectives and lax.ppermute only.
A program may use at most 64 MiB of HBM per device.

v0:
```python
import jax
import jax.numpy as jnp
from jax import lax
from jax.sharding import PartitionSpec as P

NS = 1024
ND = 4096
ITERS = 2


def local(source_fields, detector_fields, measured, valid_pair, weight_class, absorption):
    vox_count = lax.axis_size("vox")
    voxels = absorption.shape[0] * vox_count
    pred_scale = 1.0 / jnp.sqrt(jnp.float32(voxels))
    grad_scale = jnp.sqrt(jnp.float32(voxels)) / (jnp.float32(NS) * jnp.float32(ND))
    own_rows = measured.shape[0]
    maskf = valid_pair.astype(jnp.float32) / (1.0 + weight_class.astype(jnp.float32))
    mu_now = absorption
    weighted = jnp.zeros(measured.shape, jnp.float32)
    for step in range(ITERS):
        scaled = (detector_fields * mu_now[None, :]).astype(jnp.bfloat16)
        partial_pred = lax.dot_general(
            lax.all_gather(source_fields, "opt", axis=0, tiled=True),
            scaled,
            (((1,), (1,)), ((), ())),
            preferred_element_type=jnp.float32,
        )
        summed = lax.psum(partial_pred, "vox")
        predicted = lax.dynamic_slice_in_dim(summed, lax.axis_index("vox") * own_rows, own_rows, 0)
        weighted = maskf * (predicted * pred_scale - measured)
        weighted_b = weighted.astype(jnp.bfloat16)
        inner = jnp.dot(
            lax.all_gather(weighted_b, "vox", axis=0, tiled=True),
            detector_fields,
            preferred_element_type=jnp.float32,
        )
        local_grad = jnp.sum(
            inner * lax.all_gather(source_fields, "opt", axis=0, tiled=True), axis=0
        )
        gradient = lax.psum(local_grad, "opt") * grad_scale
        mu_now = jnp.maximum(mu_now - 2.0 * gradient, 0.0)
    return (mu_now, weighted)


def solution(mesh):
    placed = (
        P("opt", "vox"),
        P("opt", "vox"),
        P("vox", "opt"),
        P("vox", "opt"),
        P("vox", "opt"),
        P("vox"),
    )
    return jax.shard_map(
        local, mesh=mesh, in_specs=placed, out_specs=(P("vox"), P("vox", "opt")), check_vma=False
    )
```

profile of v0, /device:TPU:1, one launch (start us, length us, event | category | flops | bytes accessed | tf_op | source)
XLA Modules:
  0.0 953.0 jit_solution(11896403717239012675)
XLA Ops:
  7.2 0.0 all-gather.2.cloned.1.call-start
  7.2 0.7 all-gather.2.cloned.1.call-update
  7.9 0.0 copy-start.2
  7.9 0.0 copy-start.3
  7.9 0.0 copy-start.4
  7.9 0.0 all-reduce.3.cloned.1.call-start
  8.0 74.2 %all-gather.2.cloned.1.call-done = bf16[1024,768]{1,0:T(8,128)(2,1)} async-done(((bf16[64,768]{1,0:T(8,128)(2,1)}), bf16[1024,768]{1,0:T(8,128)(2,1)}) %all-gather.2.cloned.1.call-update) | async-done | bytes 1572880 | tf_op jit(solution)/shard_map/all_gather | solution.py:23
  82.2 0.0 copy-start.1
  82.2 3.2 convolution_bitcast_fusion.1
  85.4 0.0 copy-start
  85.4 0.0 all-reduce.3.cloned.1.call-update
  85.4 0.0 all-reduce.5.cloned.1.call-start
  85.5 284.5 %all-reduce.3.cloned.1.call-done = f32[1024,256]{1,0:T(8,128)} async-done(((f32[1024,256]{1,0:T(8,128)}), f32[1024,256]{1,0:T(8,128)}) %all-reduce.3.cloned.1.call-update) | async-done | bytes 1048592 | tf_op jit(solution)/shard_map/psum | solution.py:28
  370.0 0.0 copy-done.2
  370.0 0.0 copy-done.3
  370.0 0.0 copy-done.4
  370.0 0.8 multiply_convert_fusion
  370.8 66.8 %all_gather.13 = bf16[1024,256]{1,0:T(8,128)(2,1)S(1)} all-gather(bf16[32,256]{1,0:T(8,128)(2,1)S(1)} %multiply_convert_fusion), channel_id=1, replica_groups=mesh['vox'=32,'opt'=16] {'vox'}, dimensions={0}, use_global_device_ids=true | all-gather | bytes 540672 | tf_op jit(solution)/shard_map/all_gather | solution.py:33
  437.6 0.0 copy-done.1
  437.6 0.0 copy-done
  437.6 0.0 copy-start.5
  437.6 0.6 fusion
  438.2 78.6 %psum.29 = f32[768]{0:T(1024)S(1)} all-reduce(f32[768]{0:T(1024)S(1)} %fusion), channel_id=1, replica_groups=mesh['vox'=32,'opt'=16] {'opt'}, use_global_device_ids=true, to_apply=%region_2.0 | all-reduce | flops 768 | bytes 6144 | tf_op jit(solution)/shard_map/psum | solution.py:40
  516.8 0.0 copy-done.5
  516.8 1.6 convolution_bitcast_fusion
  518.5 0.0 all-reduce.5.cloned.1.call-update
  518.5 280.0 %all-reduce.5.cloned.1.call-done = f32[1024,256]{1,0:T(8,128)} async-done(((f32[1024,256]{1,0:T(8,128)}), f32[1024,256]{1,0:T(8,128)}) %all-reduce.5.cloned.1.call-update) | async-done | bytes 1048592 | tf_op jit(solution)/shard_map/psum | solution.py:28
  798.5 1.4 fusion.8
  799.9 65.8 %all_gather.14 = bf16[1024,256]{1,0:T(8,128)(2,1)S(1)} all-gather(bf16[32,256]{1,0:T(8,128)(2,1)S(1)} %get-tuple-element.6), channel_id=1, replica_groups=mesh['vox'=32,'opt'=16] {'vox'}, dimensions={0}, use_global_device_ids=true | all-gather | bytes 540672 | tf_op jit(solution)/shard_map/all_gather | solution.py:33
  865.7 0.6 fusion.1
  866.4 79.5 %psum.31 = f32[768]{0:T(1024)S(1)} all-reduce(f32[768]{0:T(1024)S(1)} %fusion.1), channel_id=1, replica_groups=mesh['vox'=32,'opt'=16] {'opt'}, use_global_device_ids=true, to_apply=%region_5.0 | all-reduce | flops 768 | bytes 6144 | tf_op jit(solution)/shard_map/psum | solution.py:40
  945.8 0.6 subtract_maximum_fusion
  (1 shorter events, 0.0 us)
Async XLA Ops:
  7.2 75.0 %all-gather.2.cloned.1.call-start = ((), (), s32[]{:S(2)}) async-start(), calls=%async_computation | async-start | bytes 1671168 | tf_op jit(solution)/shard_map/all_gather | solution.py:23
  7.9 362.1 %copy-start.2 = (f32[32,256]{1,0:T(8,128)S(1)}, f32[32,256]{1,0:T(8,128)}, u32[]{:S(2)}) copy-start(f32[32,256]{1,0:T(8,128)} %param.8) | copy-start | bytes 98308
  7.9 362.1 %copy-start.3 = (s32[32,256]{1,0:T(8,128)S(1)}, s32[32,256]{1,0:T(8,128)}, u32[]{:S(2)}) copy-start(s32[32,256]{1,0:T(8,128)} %param.10) | copy-start | bytes 98308
  7.9 362.1 %copy-start.4 = (s32[32,256]{1,0:T(8,128)S(1)}, s32[32,256]{1,0:T(8,128)}, u32[]{:S(2)}) copy-start(s32[32,256]{1,0:T(8,128)} %param.9) | copy-start | bytes 98308
  7.9 362.1 %all-reduce.3.cloned.1.call-start = ((), (), s32[]{:S(2)}) async-start(), calls=%async_computation.1 | async-start | bytes 2097152 | tf_op jit(solution)/shard_map/psum | solution.py:28
  82.2 355.4 %copy-start.1 = (bf16[256,768]{1,0:T(8,128)(2,1)S(1)}, bf16[256,768]{1,0:T(8,128)(2,1)}, u32[]{:S(2)}) copy-start(bf16[256,768]{1,0:T(8,128)(2,1)} %param.7) | copy-start | bytes 1179652
  85.4 352.2 %copy-start = (bf16[1024,768]{1,0:T(8,128)(2,1)S(1)}, bf16[1024,768]{1,0:T(8,128)(2,1)}, u32[]{:S(2)}) copy-start(bf16[1024,768]{1,0:T(8,128)(2,1)} %all-gather.2.cloned.1.call-done) | copy-start | bytes 4718596
  85.4 713.1 %all-reduce.5.cloned.1.call-start = ((), (), s32[]{:S(2)}) async-start(), calls=%async_computation.2 | async-start | bytes 2097152 | tf_op jit(solution)/shard_map/psum | solution.py:28
  437.6 79.2 %copy-start.5 = (f32[768]{0:T(1024)S(1)}, f32[768]{0:T(1024)}, u32[]{:S(2)}) copy-start(f32[768]{0:T(1024)} %param.11) | copy-start | bytes 9220
Sparse Core Ops, SparseCore 0:
  11.3 70.8 all-gather.1
  85.5 284.4 all-reduce.2
  518.6 279.8 all-reduce.4
where the time goes:
time: 953 us
  waiting for transfers between devices  639 us (67%)
  blocking collectives  291 us (31%)
  between operations  13.8 us (1%)
    psum x2, waiting for transfers between devices, local(): summed = lax.psum(partial_pred, 'vox')  565 us
    psum x2, blocking collectives, local(): gradient = lax.psum(local_grad, 'opt') * grad_scale  158 us
    all_gather x2, blocking collectives, local(): lax.all_gather(weighted_b, 'vox', axis=0, tiled=True)  133 us
    all_gather x1, waiting for transfers between devices, local(): lax.all_gather(source_fields, 'opt', axis=0, tiled=True)  74.2 us
  transfers between devices with their start and end apart: 3, of which 3 were waited for; matrix products, arithmetic and copies ran while one was open for 0% of the time, Pallas kernels for 0%

commit v1 on v0

v1 whole, which is shorter than its diff:
```python
import jax
import jax.numpy as jnp
from jax import lax
from jax.sharding import Mesh
from jax.sharding import PartitionSpec as P

NS = 1024
ND = 4096
ITERS = 2
VOX = ("z_lo", "y")
OPT = ("z_hi", "x", "core")


def everywhere(block, axes, count):
    return lax.all_to_all(jnp.broadcast_to(block[None], (count,) + block.shape), axes, 0, 0)


def gather_sources(rows):
    own, cols = rows.shape
    swapped = lax.ppermute(rows, "z_hi", [(0, 1), (1, 0)])
    low = lax.axis_index("z_hi") == 0
    both = jnp.concatenate([jnp.where(low, rows, swapped), jnp.where(low, swapped, rows)], axis=0)
    along = lax.all_gather(both, "x", axis=0)
    along = along.reshape(4, 2, own, cols)
    parts = []
    for z in range(2):
        half = lax.all_gather(along[:, z], "core", axis=1)
        parts.append(half)
    return jnp.stack(parts).reshape(16 * own, cols)


def local(source_fields, detector_fields, measured, valid_pair, weight_class, absorption):
    voxels = absorption.shape[0] * 32
    pred_scale = 1.0 / jnp.sqrt(jnp.float32(voxels))
    grad_scale = jnp.sqrt(jnp.float32(voxels)) / (jnp.float32(NS) * jnp.float32(ND))
    own_rows, own_cols = measured.shape
    maskf = valid_pair.astype(jnp.float32) / (1.0 + weight_class.astype(jnp.float32))
    sources = gather_sources(source_fields)
    mu_now = absorption
    weighted = None
    for step in range(ITERS):
        scaled = (detector_fields * mu_now[None, :]).astype(jnp.bfloat16)
        partial_pred = lax.dot_general(
            sources, scaled, (((1,), (1,)), ((), ())), preferred_element_type=jnp.float32
        )
        sent = partial_pred.astype(jnp.bfloat16).reshape(32, own_rows, own_cols)
        got = lax.all_to_all(sent, VOX, 0, 0)
        predicted = jnp.sum(got.astype(jnp.float32), axis=0)
        weighted = maskf * (predicted * pred_scale - measured)
        weighted_b = weighted.astype(jnp.bfloat16)
        all_weighted = everywhere(weighted_b, VOX, 32).reshape(32 * own_rows, own_cols)
        inner = jnp.dot(all_weighted, detector_fields, preferred_element_type=jnp.float32)
        local_grad = jnp.sum(inner * sources, axis=0)
        terms = everywhere(local_grad.reshape(6, 128), OPT, 16)
        gradient = jnp.sum(terms, axis=0).reshape(-1) * grad_scale
        mu_now = jnp.maximum(mu_now - 2.0 * gradient, 0.0)
    return (mu_now, weighted)


def solution(mesh):
    names = ("z_lo", "y", "z_hi", "x", "core")
    fine = Mesh(mesh.devices.reshape(4, 8, 2, 4, 2), names)
    placed = (P(OPT, VOX), P(OPT, VOX), P(VOX, OPT), P(VOX, OPT), P(VOX, OPT), P(VOX))
    return jax.shard_map(
        local, mesh=fine, in_specs=placed, out_specs=(P(VOX), P(VOX, OPT)), check_vma=False
    )
```

time: 953 us -> 168 us (0.18)
  waiting for transfers between devices: 639 us -> 2.29 us
  blocking collectives: 291 us -> 147 us
  between operations: 13.8 us -> 0.76 us
  starting transfers between devices: 0.12 us -> 11.5 us
    psum x2 -> x0, waiting for transfers between devices: 565 us -> none  [local(): summed = lax.psum(partial_pred, 'vox')]
    psum x2 -> x0, blocking collectives: 158 us -> none  [local(): gradient = lax.psum(local_grad, 'opt') * grad_scale]
    all_to_all x0 -> x6, blocking collectives: none -> 125 us  [the longest x4 81.3 us: everywhere(): lax.all_to_all(jnp.broadcast_to(block[None], (count,) + block.shape), axe...]
    all_gather x2 -> x3, blocking collectives: 133 us -> 22.3 us  [the longest x1 12.9 us: gather_sources(): along = lax.all_gather(both, 'x', axis=0)]
    all_gather x1 -> x0, waiting for transfers between devices: 74.2 us -> none  [local(): lax.all_gather(source_fields, 'opt', axis=0, tiled=True)]
    ppermute x0 -> x1, starting transfers between devices: none -> 11.5 us  [gather_sources(): swapped = lax.ppermute(rows, 'z_hi', [(0, 1), (1, 0)])]
  transfers between devices with their start and end apart: 3 -> 1, of which waited for: 3 -> 1; matrix products, arithmetic and copies ran while one was open for 0% -> 0% of each run, Pallas kernels for 0% -> 0%
where the time goes in v1:
time: 168 us; the launch traced here: 167 us
  blocking collectives  147 us (88%)
  starting transfers between devices  11.5 us (7%)
  other arithmetic  2.54 us (2%)
  matrix products  2.47 us (1%)
  waiting for transfers between devices  2.29 us (1%)
    all_to_all x4, blocking collectives, everywhere(): lax.all_to_all(jnp.broadcast_to(block[None], (count,) + block.shape), axe...  81.3 us
    all_to_all x2, blocking collectives, local(): got = lax.all_to_all(sent, VOX, 0, 0)  43.3 us
    all_gather x1, blocking collectives, gather_sources(): along = lax.all_gather(both, 'x', axis=0)  12.9 us
    ppermute x1, starting transfers between devices, gather_sources(): swapped = lax.ppermute(rows, 'z_hi', [(0, 1), (1, 0)])  11.5 us
    all_gather x2, blocking collectives, gather_sources(): half = lax.all_gather(along[:, z], 'core', axis=1)  9.46 us
  transfers between devices with their start and end apart: 1, of which 1 were waited for; matrix products, arithmetic and copies ran while one was open for 0% of the time, Pallas kernels for 0%

profile of v1, /device:TPU:1, one launch (start us, length us, event | category | flops | bytes accessed | tf_op | source)
XLA Modules:
  0.0 167.5 jit_solution(7332507388491761052)
XLA Ops:
  0.6 11.5 %collective-permute-start = (bf16[64,768]{1,0:T(8,128)(2,1)}, bf16[64,768]{1,0:T(8,128)(2,1)S(1)}, u32[]{:S(2)}, u32[]{:S(2)}) collective-permute-start(bf16[64,768]{1,0:T(8,128)(2,1)} %param.6), channel_id=1, source_target_pairs={{0,8},{8,0},{1,9},{9,1},{2,10},{10,2},{3,11},{11,3},{4,12},{12,4},... | collective-permute-start | bytes 294920 | tf_op jit(solution)/shard_map/ppermute | solution.py:20
  12.1 2.3 %collective-permute-done = bf16[64,768]{1,0:T(8,128)(2,1)S(1)} collective-permute-done((bf16[64,768]{1,0:T(8,128)(2,1)}, bf16[64,768]{1,0:T(8,128)(2,1)S(1)}, u32[]{:S(2)}, u32[]{:S(2)}) %collective-permute-start) | collective-permute-done | bytes 98336 | tf_op jit(solution)/shard_map/ppermute | solution.py:20
  14.4 0.9 broadcast_select_fusion.1
  15.3 12.9 %all-gather = bf16[512,768]{1,0:T(8,128)(2,1)S(1)} all-gather(bf16[128,768]{1,0:T(8,128)(2,1)S(1)} %pad_maximum_fusion.1), channel_id=2, replica_groups=mesh['z_lo'=4,'y'=8,'z_hi'=2,'x'=4,'core'=2] {'x'}, dimensions={0}, use_global_device_ids=true | all-gather | bytes 983040 | tf_op jit(solution)/shard_map/all_gather | solution.py:23
  28.2 0.1 fusion.11
  28.3 7.1 %all_gather.14 = bf16[4,2,64,768]{3,2,1,0:T(8,128)(2,1)S(1)} all-gather(bf16[4,1,64,768]{3,2,1,0:T(8,128)(2,1)S(1)} %get-tuple-element.4), channel_id=1, replica_groups=mesh['z_lo'=4,'y'=8,'z_hi'=2,'x'=4,'core'=2] {'core'}, dimensions={1}, use_global_device_ids=true | all-gather | bytes 1179648 | tf_op jit(solution)/shard_map/all_gather | solution.py:27
  35.4 2.4 %all_gather.15 = bf16[4,2,64,768]{3,2,1,0:T(8,128)(2,1)S(1)} all-gather(bf16[4,1,64,768]{3,2,1,0:T(8,128)(2,1)S(1)} %get-tuple-element.5), channel_id=1, replica_groups=mesh['z_lo'=4,'y'=8,'z_hi'=2,'x'=4,'core'=2] {'core'}, dimensions={1}, use_global_device_ids=true | all-gather | bytes 1179648 | tf_op jit(solution)/shard_map/all_gather | solution.py:27
  37.7 0.0 copy-start.3
  37.7 0.0 copy-start.4
  37.7 0.1 pad_maximum_fusion
  37.9 0.5 copy-done.3
  38.4 0.3 copy-done.4
  38.7 0.0 copy-start
  38.7 0.0 copy-start.1
  38.7 0.6 convolution_convert_fusion.1
  39.4 23.5 %all_to_all.30 = bf16[32,32,256]{2,1,0:T(8,128)(2,1)S(1)} all-to-all(bf16[32,32,256]{2,1,0:T(8,128)(2,1)S(1)} %bitcast.33), channel_id=1, replica_groups=mesh['z_lo'=4,'y'=8,'z_hi'=2,'x'=4,'core'=2] {'z_lo','y'}, dimensions={0} | all-to-all | bytes 1048576 | tf_op jit(solution)/shard_map/all_to_all | solution.py:47
  62.9 0.1 convert_reduce_fusion.1
  63.0 0.0 copy-done
  63.0 0.0 copy-done.1
  63.0 0.0 copy-done.2
  63.0 0.1 broadcast_in_dim.12
  63.1 22.1 %all_to_all.31 = bf16[32,32,256]{2,1,0:T(8,128)(2,1)S(1)} all-to-all(bf16[32,32,256]{2,1,0:T(8,128)(2,1)S(1)} %broadcast_in_dim.12), channel_id=1, replica_groups=mesh['z_lo'=4,'y'=8,'z_hi'=2,'x'=4,'core'=2] {'z_lo','y'}, dimensions={0} | all-to-all | bytes 1048576 | tf_op jit(solution)/shard_map/all_to_all | solution.py:15
  85.2 0.6 fusion
  85.8 21.8 %all_to_all.32 = f32[16,6,128]{2,1,0:T(8,128)S(1)} all-to-all(f32[16,6,128]{2,1,0:T(8,128)S(1)} %broadcast_in_dim.14), channel_id=1, replica_groups=mesh['z_lo'=4,'y'=8,'z_hi'=2,'x'=4,'core'=2] {'z_hi','x','core'}, dimensions={0} | all-to-all | bytes 98304 | tf_op jit(solution)/shard_map/all_to_all | solution.py:15
  107.7 0.6 convolution_convert_fusion
  108.3 19.7 %all_to_all.33 = bf16[32,32,256]{2,1,0:T(8,128)(2,1)S(1)} all-to-all(bf16[32,32,256]{2,1,0:T(8,128)(2,1)S(1)} %bitcast.34), channel_id=1, replica_groups=mesh['z_lo'=4,'y'=8,'z_hi'=2,'x'=4,'core'=2] {'z_lo','y'}, dimensions={0} | all-to-all | bytes 1048576 | tf_op jit(solution)/shard_map/all_to_all | solution.py:47
  128.0 0.1 convert_reduce_fusion
  128.1 0.6 fusion.10
  128.8 21.8 %all_to_all.34 = bf16[32,32,256]{2,1,0:T(8,128)(2,1)S(1)} all-to-all(bf16[32,32,256]{2,1,0:T(8,128)(2,1)S(1)} %broadcast_in_dim.15), channel_id=1, replica_groups=mesh['z_lo'=4,'y'=8,'z_hi'=2,'x'=4,'core'=2] {'z_lo','y'}, dimensions={0} | all-to-all | bytes 1048576 | tf_op jit(solution)/shard_map/all_to_all | solution.py:15
  150.6 0.6 fusion.1
  151.2 15.7 %all_to_all.35 = f32[16,6,128]{2,1,0:T(8,128)S(1)} all-to-all(f32[16,6,128]{2,1,0:T(8,128)S(1)} %broadcast_in_dim.33), channel_id=1, replica_groups=mesh['z_lo'=4,'y'=8,'z_hi'=2,'x'=4,'core'=2] {'z_hi','x','core'}, dimensions={0} | all-to-all | bytes 98304 | tf_op jit(solution)/shard_map/all_to_all | solution.py:15
  166.9 0.6 fusion.8
  (9 shorter events, 0.1 us)
Async XLA Ops:
  0.6 13.8 %collective-permute-start = (bf16[64,768]{1,0:T(8,128)(2,1)}, bf16[64,768]{1,0:T(8,128)(2,1)S(1)}, u32[]{:S(2)}, u32[]{:S(2)}) collective-permute-start(bf16[64,768]{1,0:T(8,128)(2,1)} %param.6), channel_id=1, source_target_pairs={{0,8},{8,0},{1,9},{9,1},{2,10},{10,2},{3,11},{11,3},{4,12},{12,4},... | collective-permute-start | bytes 294920 | tf_op jit(solution)/shard_map/ppermute | solution.py:20
  37.7 0.7 copy-start.3
  37.7 1.0 copy-start.4
  38.7 24.2 %copy-start = (f32[32,256]{1,0:T(8,128)S(1)}, f32[32,256]{1,0:T(8,128)}, u32[]{:S(2)}) copy-start(f32[32,256]{1,0:T(8,128)} %param.8) | copy-start | bytes 98308
  38.7 24.3 %copy-start.1 = (s32[32,256]{1,0:T(8,128)S(1)}, s32[32,256]{1,0:T(8,128)}, u32[]{:S(2)}) copy-start(s32[32,256]{1,0:T(8,128)} %param.10) | copy-start | bytes 98308
  38.7 24.3 %copy-start.2 = (s32[32,256]{1,0:T(8,128)S(1)}, s32[32,256]{1,0:T(8,128)}, u32[]{:S(2)}) copy-start(s32[32,256]{1,0:T(8,128)} %param.9) | copy-start | bytes 98308
